TPU v7x, 1024 devices: a whole 8x8x8 slice. The times are simulated.
1024 devices in a mesh: vel: 16 (over y_lo, x), space: 64 (over y_hi, z, core).
Axes of the slice: x: 8, y: 8 (y_hi: 4, y_lo: 2; y = y_hi * 2 + y_lo), z: 8, core: 2. Of those that a mesh axis runs over, the one named last changes fastest.
Arguments:
- distribution: float32 [2304, 256, 256], P('vel', 'space'), may hold values from -3 to 3
- moments_old: float32 [10, 256, 256], P(None, 'space'), may hold values from -6 to 6
- pore_mask: int32 [256, 256], P('space'), may hold values 0 or 1
- synthetic_rate: float32 [10], replicated, may hold values from 0.2 to 4
Outputs:
- distribution_new: float32 [2304, 256, 256], P('vel', 'space')
- moments_new: float32 [10, 256, 256], P(None, 'space')
Inputs may be any that keep to these rules, and one draw needn't show every extreme that they name: `pore_mask`: 1 marks a pore cell, 0 a solid one.
All inputs are finite; a program needn't handle non-finite values. No bound on the sum of `pore_mask` on one device may be relied on, other than what follows from the above.
Results may differ from a plain program's by a relative error of at most 0.000092.
Values sent between devices are 32-bit elements; how exact they have to be, the bound alone decides.
No kernel may reach another device: no remote copies, remote signals or barrier semaphores. Data moves between devices by JAX's collectives and lax.ppermute only.
A program may use at most 32 MiB of HBM per device.

v0:
```python
import math

import jax
import jax.numpy as jnp
from jax import lax
from jax.sharding import PartitionSpec as P

VX = 16
VY = 12
VZ = 12
NY = 16
NZ = 16
TSWEEPS = 2
SWEEPS = 5


extent = 3.0
collide = 1.0
coefficients = (1.0, 2.0, 2.0, 2.0, 0.6667, 0.8, 0.8, 0.8, 2.0, 2.0)


def padded_2(cells, sides, width):
    for axis, dim in sides:
        count = lax.axis_size(axis)
        head = lax.slice_in_dim(cells, 0, width, axis=dim)
        tail = lax.slice_in_dim(cells, cells.shape[dim] - width, cells.shape[dim], axis=dim)
        cells = jnp.concatenate(
            [
                lax.ppermute(tail, axis, [(i, (i + 1) % count) for i in range(count)]),
                cells,
                lax.ppermute(head, axis, [((i + 1) % count, i) for i in range(count)]),
            ],
            axis=dim,
        )
    return cells


def from_everyone(array, axis):
    copies = jnp.broadcast_to(array, (lax.axis_size(axis), *array.shape))
    return lax.all_to_all(copies, axis, split_axis=0, concat_axis=0, tiled=True)


def over_copies(array, axis):
    everything = from_everyone(array, axis)
    return jnp.sum(everything, axis=0)


def node_values(indices, count):
    return -extent + (indices.astype(jnp.float32) + 0.5) * (2.0 * extent / count)


def velocity_tables(first_group, groups, along_x, along_y, along_z):
    first_nodes = node_values(first_group + jnp.arange(groups, dtype=jnp.int32), along_x)
    second_nodes = node_values(jnp.arange(along_y, dtype=jnp.int32), along_y)
    third_nodes = node_values(jnp.arange(along_z, dtype=jnp.int32), along_z)
    block_shape = (groups, along_y, along_z)
    speed_one = jnp.broadcast_to(first_nodes[:, None, None], block_shape).reshape(-1)
    speed_two = jnp.broadcast_to(second_nodes[None, :, None], block_shape).reshape(-1)
    speed_three = jnp.broadcast_to(third_nodes[None, None, :], block_shape).reshape(-1)
    energy = speed_one * speed_one + speed_two * speed_two + speed_three * speed_three
    functions = jnp.stack(
        [
            jnp.ones_like(energy),
            speed_one,
            speed_two,
            speed_three,
            energy - 1.5,
            speed_one * (energy - 2.5),
            speed_two * (energy - 2.5),
            speed_three * (energy - 2.5),
            speed_one * speed_two,
            speed_two * speed_three,
        ]
    )
    volume = (2.0 * extent) ** 3 / (along_x * along_y * along_z) / math.pi**1.5
    moment_rows = functions * volume
    factors = jnp.array(coefficients, dtype=jnp.float32)
    spread_rows = jnp.transpose(functions * factors[:, None] * jnp.exp(-energy)[None, :])
    return ((speed_one, speed_two, speed_three), moment_rows, spread_rows)


def upwind_sweep(padded, source, porous, speeds, along_y, along_z):
    speed_one, speed_two, speed_three = speeds
    middle = padded[:, 1:-1]
    groups, thickness, plane_cells = middle.shape
    cube_view = middle.reshape(groups, thickness, along_y, along_z)
    from_first = jnp.where(speed_one[:, None, None] > 0, padded[:, :-2], padded[:, 2:])
    from_second = jnp.where(
        speed_two[:, None, None, None] > 0, jnp.roll(cube_view, 1, 2), jnp.roll(cube_view, -1, 2)
    )
    from_third = jnp.where(
        speed_three[:, None, None, None] > 0, jnp.roll(cube_view, 1, 3), jnp.roll(cube_view, -1, 3)
    )
    across = (
        jnp.abs(speed_two)[:, None, None, None] * from_second
        + jnp.abs(speed_three)[:, None, None, None] * from_third
    )
    inflow = jnp.abs(speed_one)[:, None, None] * from_first + across.reshape(
        groups, thickness, plane_cells
    )
    denominator = collide + jnp.abs(speed_one) + jnp.abs(speed_two) + jnp.abs(speed_three)
    return porous[None] * (collide * source + inflow) / denominator[:, None, None]


def relax_step(padded, forcing, porous, rates, along_y, along_z):
    middle = padded[:, 1:-1]
    moment_count, thickness, plane_cells = middle.shape
    cube_view = middle.reshape(moment_count, thickness, along_y, along_z)
    beside = (
        jnp.roll(cube_view, 1, 2)
        + jnp.roll(cube_view, -1, 2)
        + jnp.roll(cube_view, 1, 3)
        + jnp.roll(cube_view, -1, 3)
    )
    neighbours = (
        padded[:, :-2] + padded[:, 2:] + beside.reshape(moment_count, thickness, plane_cells)
    )
    return porous[None] * (forcing + neighbours) / (rates + 6.0)[:, None, None]


def lift(spread_rows, fields):
    moment_count = fields.shape[0]
    flat = jnp.dot(
        spread_rows,
        fields.reshape(moment_count, -1),
        precision=lax.Precision.HIGHEST,
        preferred_element_type=jnp.float32,
    )
    return flat.reshape(spread_rows.shape[0], fields.shape[1], fields.shape[2])


def body(distribution, moments_old, pore_mask, synthetic_rate):
    porous = pore_mask.astype(jnp.float32)
    velocities, thickness, plane_cells = distribution.shape
    moment_count = moments_old.shape[0]
    local_groups = velocities // (VY * VZ)
    first_group = lax.axis_index("vel") * local_groups
    speeds, moment_rows, spread_rows = velocity_tables(first_group, local_groups, VX, VY, VZ)
    current = padded_2(distribution, (("space", 1),), TSWEEPS)
    stacked = jnp.concatenate([moments_old, porous[None]], axis=0)
    widened = padded_2(stacked, (("space", 1),), TSWEEPS - 1)
    wide_source = lift(spread_rows, widened[:moment_count])
    wide_porous = widened[moment_count]
    for sweep_number in range(TSWEEPS):
        inner_cells = current.shape[1] - 2
        current = upwind_sweep(
            current,
            wide_source[:, sweep_number : sweep_number + inner_cells],
            wide_porous[sweep_number : sweep_number + inner_cells],
            speeds,
            NY,
            NZ,
        )
    partial_value = jnp.dot(
        moment_rows,
        current.reshape(velocities, -1),
        precision=lax.Precision.HIGHEST,
        preferred_element_type=jnp.float32,
    ).reshape(moment_count, thickness, plane_cells)
    moments_half = over_copies(partial_value, "vel")
    change = moments_half - moments_old
    denominators = (synthetic_rate + 6.0)[:, None, None]
    reach_cells = SWEEPS - 1
    stacked = jnp.concatenate([change, porous[None]], axis=0)
    widened = padded_2(stacked, (("space", 1),), reach_cells)
    wide_change = widened[:moment_count]
    wide_porous = widened[moment_count]
    correction = wide_porous[None] * wide_change / denominators
    for sweep_number in range(reach_cells):
        inner_cells = correction.shape[1] - 2
        offset = sweep_number + 1
        correction = relax_step(
            correction,
            wide_change[:, offset : offset + inner_cells],
            wide_porous[offset : offset + inner_cells],
            synthetic_rate,
            NY,
            NZ,
        )
    moments_new = moments_half + correction
    distribution_new = current + porous[None] * lift(spread_rows, correction)
    return (distribution_new, moments_new)


def solution(mesh):
    placed = (P("vel", "space", None), P(None, "space", None), P("space", None), P())
    return jax.shard_map(
        body,
        mesh=mesh,
        in_specs=placed,
        out_specs=(P("vel", "space", None), P(None, "space", None)),
        check_vma=False,
    )
```

profile of v0, /device:TPU:2, one launch (start us, length us, event | category | flops | bytes accessed | tf_op | source)
XLA Modules:
  0.0 112.1 jit_solution(4381343841628215620)
XLA Ops:
  0.7 1.2 %copy.68 = f32[144,4,256]{2,0,1:T(8,128)S(1)} copy(f32[144,4,256]{2,1,0:T(4,128)} %param.5) | data formatting | bytes 1179648 | tf_op args[0]
  2.8 1.9 %collective-permute-start.2 = (f32[144,2,256]{2,0,1:T(8,128)S(1)}, f32[144,2,256]{2,0,1:T(8,128)S(1)}, u32[]{:S(2)}, u32[]{:S(2)}) collective-permute-start(f32[144,2,256]{2,0,1:T(8,128)S(1)} %get-tuple-element.47), channel_id=1, source_target_pairs={{0,1},{1,2},{2,3},{3,4},{4,5},{5,6},{6,7},{7,8},{8,9},{9,10},{10,1... | collective-permute-start | bytes 884744 | tf_op jit(solution)/shard_map/ppermute | solution.py:29
  4.7 21.1 %collective-permute-start.3 = (f32[144,2,256]{2,0,1:T(8,128)S(1)}, f32[144,2,256]{2,0,1:T(8,128)S(1)}, u32[]{:S(2)}, u32[]{:S(2)}) collective-permute-start(f32[144,2,256]{2,0,1:T(8,128)S(1)} %get-tuple-element.46), channel_id=1, source_target_pairs={{1,0},{2,1},{3,2},{4,3},{5,4},{6,5},{7,6},{8,7},{9,8},{10,9},{11,1... | collective-permute-start | bytes 884744 | tf_op jit(solution)/shard_map/ppermute | solution.py:31
  25.9 2.6 %collective-permute-start.1 = (f32[11,1,256]{2,1,0:T(1,128)S(1)}, f32[11,1,256]{2,1,0:T(1,128)S(1)}, u32[]{:S(2)}, u32[]{:S(2)}) collective-permute-start(f32[11,1,256]{2,1,0:T(1,128)S(1)} %get-tuple-element.65), channel_id=1, source_target_pairs={{1,0},{2,1},{3,2},{4,3},{5,4},{6,5},{7,6},{8,7},{9,8},{10,9},{11,1... | collective-permute-start | bytes 33800 | tf_op jit(solution)/shard_map/ppermute | solution.py:31
  28.5 1.9 %collective-permute-start = (f32[11,1,256]{2,1,0:T(1,128)S(1)}, f32[11,1,256]{2,1,0:T(1,128)S(1)}, u32[]{:S(2)}, u32[]{:S(2)}) collective-permute-start(f32[11,1,256]{2,1,0:T(1,128)S(1)} %get-tuple-element.64), channel_id=1, source_target_pairs={{0,1},{1,2},{2,3},{3,4},{4,5},{5,6},{6,7},{7,8},{8,9},{9,10},{10,1... | collective-permute-start | bytes 33800 | tf_op jit(solution)/shard_map/ppermute | solution.py:29
  31.9 1.6 %collective-permute-done.1 = f32[11,1,256]{2,1,0:T(1,128)S(1)} collective-permute-done((f32[11,1,256]{2,1,0:T(1,128)S(1)}, f32[11,1,256]{2,1,0:T(1,128)S(1)}, u32[]{:S(2)}, u32[]{:S(2)}) %collective-permute-start.1) | collective-permute-done | bytes 11296 | tf_op jit(solution)/shard_map/ppermute | solution.py:31
  33.5 4.2 %collective-permute-done = f32[11,1,256]{2,1,0:T(1,128)S(1)} collective-permute-done((f32[11,1,256]{2,1,0:T(1,128)S(1)}, f32[11,1,256]{2,1,0:T(1,128)S(1)}, u32[]{:S(2)}, u32[]{:S(2)}) %collective-permute-start) | collective-permute-done | bytes 11296 | tf_op jit(solution)/shard_map/ppermute | solution.py:29
  40.5 2.0 %fusion.65 = (f32[144,6,15,16]{0,3,2,1:T(8,128)}, f32[144,6,15,16]{0,3,2,1:T(8,128)}) fusion(f32[144,6,16,16]{0,3,2,1:T(8,128)S(1)} %bitcast.71), kind=kLoop, calls=%fused_computation.110 | loop fusion | bytes 3317760 | tf_op jit(solution)/shard_map/jit(_roll_static)/slice | solution.py:89
  43.1 1.4 %copy.77 = f32[144,6,256]{2,0,1:T(8,128)} copy(f32[144,6,256]{0,2,1:T(8,128)S(1)} %bitcast.79) | data formatting | bytes 1769472 | tf_op jit(solution)/shard_map/jit(_roll_static)/concatenate | solution.py:92
  44.4 1.4 %copy.78 = f32[144,6,256]{2,0,1:T(8,128)} copy(f32[144,6,256]{0,2,1:T(8,128)S(1)} %bitcast.77) | data formatting | bytes 1769472 | tf_op jit(solution)/shard_map/jit(_roll_static)/concatenate | solution.py:92
  45.8 2.4 %pad_maximum_fusion.2 = (f32[144,6,16,16]{0,3,2,1:T(8,128)S(1)}, f32[144,6,16,16]{0,3,2,1:T(8,128)S(1)}) fusion(f32[144,6,15,16]{0,3,2,1:T(8,128)} %get-tuple-element.15, f32[144,6,1,16]{0,3,2,1:T(8,128)S(1)} %get-tuple-element.17, f32[144,6,1,16]{0,3,2,1:T(8,128)S(1)} %get-tuple-element.16, f32[144,6,15,16]{0,3,2,1:T(8,128)} %get-tuple-element.14), kind=kLoop, calls=%fused_computation.2 | loop fusion | flops 442368 | bytes 3538944 | tf_op jit(solution)/shard_map/jit(_roll_static)/concatenate | solution.py:89
  48.1 1.4 %copy.75 = f32[144,6,256]{2,0,1:T(8,128)} copy(f32[144,6,256]{0,2,1:T(8,128)S(1)} %bitcast.80) | data formatting | bytes 1769472 | tf_op jit(solution)/shard_map/jit(_roll_static)/concatenate | solution.py:89
  49.6 1.4 %copy.76 = f32[144,6,256]{2,0,1:T(8,128)} copy(f32[144,6,256]{0,2,1:T(8,128)S(1)} %bitcast.78) | data formatting | bytes 1769472 | tf_op jit(solution)/shard_map/jit(_roll_static)/concatenate | solution.py:89
  51.1 4.0 %fusion.5 = (f32[144,6,256]{2,0,1:T(8,128)S(1)}, f32[144,6,256]{2,0,1:T(8,128)}) fusion(f32[144,4,256]{2,0,1:T(8,128)S(1)} %copy-done.5, f32[144,2,256]{2,0,1:T(8,128)S(1)} %copy-done.10, f32[144,2,256]{2,0,1:T(8,128)} %copy-done.11, f32[144,6,256]{2,0,1:T(8,128)S(1)} %copy-done.7, f32[144,6,256]{2,0,1:T(8,128)} %copy.78, f32[144,6,256]{2,0,1:T(8,128)} %copy.75, ...), kind=kOutput, calls=%fused_computation.17 | convolution fusion | flops 29420352 | bytes 6564045 | tf_op jit(solution)/shard_map/dot_general | solution.py:123
  56.7 1.2 %fusion.69 = (f32[144,4,15,16]{0,3,2,1:T(8,128)S(1)}, f32[144,4,15,16]{0,3,2,1:T(8,128)}) fusion(f32[144,4,16,16]{0,3,2,1:T(8,128)S(1)} %bitcast.75), kind=kLoop, calls=%fused_computation.114 | loop fusion | bytes 2211840 | tf_op jit(solution)/shard_map/jit(_roll_static)/slice | solution.py:89
  59.4 1.1 %copy.83 = f32[144,4,256]{2,0,1:T(8,128)} copy(f32[144,4,256]{0,2,1:T(8,128)S(1)} %bitcast.82) | data formatting | bytes 1179648 | tf_op jit(solution)/shard_map/jit(_roll_static)/concatenate | solution.py:92
  60.7 1.1 %copy.80 = f32[144,4,256]{2,0,1:T(8,128)} copy(f32[144,4,256]{0,2,1:T(8,128)S(1)} %bitcast.83) | data formatting | bytes 1179648 | tf_op jit(solution)/shard_map/jit(_roll_static)/concatenate | solution.py:89
  62.0 1.1 %copy.81 = f32[144,4,256]{2,0,1:T(8,128)} copy(f32[144,4,256]{0,2,1:T(8,128)S(1)} %bitcast.84) | data formatting | bytes 1179648 | tf_op jit(solution)/shard_map/jit(_roll_static)/concatenate | solution.py:89
  63.5 1.9 %fusion.17 = f32[144,4,256]{2,0,1:T(8,128)S(1)} fusion(f32[144,6,256]{2,0,1:T(8,128)S(1)} %copy-done.2, f32[144,6,256]{2,0,1:T(8,128)} %get-tuple-element.74, f32[144,4,256]{2,0,1:T(8,128)S(1)} %copy-done.6, f32[144,4,256]{2,0,1:T(8,128)} %copy.83, f32[144,4,256]{2,0,1:T(8,128)} %copy.80, f32[144,4,256]{2,0,1:T(8,128)} %copy.81, f32[144]{0:T(256)S(1)} %add_add_fusion, ...), kind=kLoop, calls=%fused_computation.32 | loop fusion | flops 1622016 | bytes 4724709 | tf_op jit(solution)/shard_map/div | solution.py:102
  66.0 21.1 %all_to_all.5 = f32[16,10,4,256]{3,2,1,0:T(4,128)S(1)} all-to-all(f32[16,10,4,256]{3,2,1,0:T(4,128)S(1)} %broadcast_in_dim.159), channel_id=1, replica_groups=mesh['vel'=16,'space'=64] {'vel'}, dimensions={0} | all-to-all | bytes 1310720 | tf_op jit(solution)/shard_map/all_to_all | solution.py:40
  87.2 5.6 %collective-permute-start.5 = (f32[11,4,256]{2,1,0:T(4,128)S(1)}, f32[11,4,256]{2,1,0:T(4,128)S(1)}, u32[]{:S(2)}, u32[]{:S(2)}) collective-permute-start(f32[11,4,256]{2,1,0:T(4,128)S(1)} %pad_maximum_fusion.12), channel_id=1, source_target_pairs={{1,0},{2,1},{3,2},{4,3},{5,4},{6,5},{7,6},{8,7},{9,8},{10,9},{11,1... | collective-permute-start | bytes 135176 | tf_op jit(solution)/shard_map/ppermute | solution.py:31
  92.8 2.1 %collective-permute-start.4 = (f32[11,4,256]{2,1,0:T(4,128)S(1)}, f32[11,4,256]{2,1,0:T(4,128)S(1)}, u32[]{:S(2)}, u32[]{:S(2)}) collective-permute-start(f32[11,4,256]{2,1,0:T(4,128)S(1)} %pad_maximum_fusion.12), channel_id=1, source_target_pairs={{0,1},{1,2},{2,3},{3,4},{4,5},{5,6},{6,7},{7,8},{8,9},{9,10},{10,1... | collective-permute-start | bytes 135176 | tf_op jit(solution)/shard_map/ppermute | solution.py:29
  94.9 7.5 %collective-permute-done.4 = f32[11,4,256]{2,1,0:T(4,128)S(1)} collective-permute-done((f32[11,4,256]{2,1,0:T(4,128)S(1)}, f32[11,4,256]{2,1,0:T(4,128)S(1)}, u32[]{:S(2)}, u32[]{:S(2)}) %collective-permute-start.4) | collective-permute-done | bytes 45088 | tf_op jit(solution)/shard_map/ppermute | solution.py:29
  110.9 1.2 %copy.89 = f32[144,4,256]{2,1,0:T(4,128)} copy(f32[144,4,256]{2,0,1:T(8,128)S(1)} %fusion) | data formatting | bytes 1179648
  (139 shorter events, 18.3 us)
Async XLA Ops:
  0.6 30.5 %copy-start.3 = (f32[144,4,256]{2,1,0:T(4,128)S(1)}, f32[144,4,256]{2,1,0:T(4,128)}, u32[]{:S(2)}) copy-start(f32[144,4,256]{2,1,0:T(4,128)} %param.5) | copy-start | bytes 1769476
  0.6 25.2 %copy-start.13 = (s32[4,256]{1,0:T(4,128)S(1)}, s32[4,256]{1,0:T(4,128)}, u32[]{:S(2)}) copy-start(s32[4,256]{1,0:T(4,128)} %param.7) | copy-start | bytes 12292
  0.6 25.2 %copy-start.8 = (f32[10,4,256]{2,1,0:T(4,128)S(1)}, f32[10,4,256]{2,1,0:T(4,128)}, u32[]{:S(2)}) copy-start(f32[10,4,256]{2,1,0:T(4,128)} %param.6) | copy-start | bytes 122884
  1.9 0.8 copy-start.4
  2.8 36.4 %collective-permute-start.2 = (f32[144,2,256]{2,0,1:T(8,128)S(1)}, f32[144,2,256]{2,0,1:T(8,128)S(1)}, u32[]{:S(2)}, u32[]{:S(2)}) collective-permute-start(f32[144,2,256]{2,0,1:T(8,128)S(1)} %get-tuple-element.47), channel_id=1, source_target_pairs={{0,1},{1,2},{2,3},{3,4},{4,5},{5,6},{6,7},{7,8},{8,9},{9,10},{10,1... | collective-permute-start | bytes 884744 | tf_op jit(solution)/shard_map/ppermute | solution.py:29
  4.7 33.8 %collective-permute-start.3 = (f32[144,2,256]{2,0,1:T(8,128)S(1)}, f32[144,2,256]{2,0,1:T(8,128)S(1)}, u32[]{:S(2)}, u32[]{:S(2)}) collective-permute-start(f32[144,2,256]{2,0,1:T(8,128)S(1)} %get-tuple-element.46), channel_id=1, source_target_pairs={{1,0},{2,1},{3,2},{4,3},{5,4},{6,5},{7,6},{8,7},{9,8},{10,9},{11,1... | collective-permute-start | bytes 884744 | tf_op jit(solution)/shard_map/ppermute | solution.py:31
  25.9 7.6 %collective-permute-start.1 = (f32[11,1,256]{2,1,0:T(1,128)S(1)}, f32[11,1,256]{2,1,0:T(1,128)S(1)}, u32[]{:S(2)}, u32[]{:S(2)}) collective-permute-start(f32[11,1,256]{2,1,0:T(1,128)S(1)} %get-tuple-element.65), channel_id=1, source_target_pairs={{1,0},{2,1},{3,2},{4,3},{5,4},{6,5},{7,6},{8,7},{9,8},{10,9},{11,1... | collective-permute-start | bytes 33800 | tf_op jit(solution)/shard_map/ppermute | solution.py:31
  28.5 9.2 %collective-permute-start = (f32[11,1,256]{2,1,0:T(1,128)S(1)}, f32[11,1,256]{2,1,0:T(1,128)S(1)}, u32[]{:S(2)}, u32[]{:S(2)}) collective-permute-start(f32[11,1,256]{2,1,0:T(1,128)S(1)} %get-tuple-element.64), channel_id=1, source_target_pairs={{0,1},{1,2},{2,3},{3,4},{4,5},{5,6},{6,7},{7,8},{8,9},{9,10},{10,1... | collective-permute-start | bytes 33800 | tf_op jit(solution)/shard_map/ppermute | solution.py:29
  38.5 0.7 copy-start.11
  39.2 0.8 copy-start.9
  49.5 1.4 %copy-start.5 = (f32[144,4,256]{2,0,1:T(8,128)S(1)}, f32[144,4,256]{2,0,1:T(8,128)}, u32[]{:S(2)}) copy-start(f32[144,4,256]{2,0,1:T(8,128)} %copy-done.4) | copy-start | bytes 1769476
  49.5 1.4 %copy-start.7 = (f32[144,6,256]{2,0,1:T(8,128)S(1)}, f32[144,6,256]{2,0,1:T(8,128)}, u32[]{:S(2)}) copy-start(f32[144,6,256]{2,0,1:T(8,128)} %copy.77) | copy-start | bytes 2654212
  49.5 1.5 %copy-start.10 = (f32[144,2,256]{2,0,1:T(8,128)S(1)}, f32[144,2,256]{2,0,1:T(8,128)}, u32[]{:S(2)}) copy-start(f32[144,2,256]{2,0,1:T(8,128)} %copy-done.9) | copy-start | bytes 884740
  49.5 1.6 %copy-start.12 = (f32[6,256,10]{1,0,2:T(8,128)S(1)}, f32[6,256,10]{1,0,2:T(8,128)}, u32[]{:S(2)}) copy-start(f32[6,256,10]{1,0,2:T(8,128)} %dot_general.22) | copy-start | bytes 184324
  49.5 1.6 %copy-start.14 = (f32[10]{0:T(128)S(1)}, f32[10]{0:T(128)}, u32[]{:S(2)}) copy-start(f32[10]{0:T(128)} %constant.36.clone) | copy-start | bytes 124
  55.1 0.9 copy-start.1
  59.4 1.2 %copy-start = (f32[144,4,15,16]{0,3,2,1:T(8,128)S(1)}, f32[144,4,15,16]{0,3,2,1:T(8,128)}, u32[]{:S(2)}) copy-start(f32[144,4,15,16]{0,3,2,1:T(8,128)} %get-tuple-element.23) | copy-start | bytes 1658884
  62.0 1.2 %copy-start.2 = (f32[144,6,256]{2,0,1:T(8,128)S(1)}, f32[144,6,256]{2,0,1:T(8,128)}, u32[]{:S(2)}) copy-start(f32[144,6,256]{2,0,1:T(8,128)} %copy-done.1) | copy-start | bytes 2654212
  62.0 1.5 %copy-start.6 = (f32[144,4,256]{2,0,1:T(8,128)S(1)}, f32[144,4,256]{2,0,1:T(8,128)}, u32[]{:S(2)}) copy-start(f32[144,4,256]{2,0,1:T(8,128)} %copy.82) | copy-start | bytes 1769476
  65.8 29.1 %copy-start.15 = (f32[10]{0:T(128)S(1)}, f32[10]{0:T(128)}, u32[]{:S(2)}) copy-start(f32[10]{0:T(128)} %param.8) | copy-start | bytes 124
  87.2 7.7 %collective-permute-start.5 = (f32[11,4,256]{2,1,0:T(4,128)S(1)}, f32[11,4,256]{2,1,0:T(4,128)S(1)}, u32[]{:S(2)}, u32[]{:S(2)}) collective-permute-start(f32[11,4,256]{2,1,0:T(4,128)S(1)} %pad_maximum_fusion.12), channel_id=1, source_target_pairs={{1,0},{2,1},{3,2},{4,3},{5,4},{6,5},{7,6},{8,7},{9,8},{10,9},{11,1... | collective-permute-start | bytes 135176 | tf_op jit(solution)/shard_map/ppermute | solution.py:31
  92.8 9.6 %collective-permute-start.4 = (f32[11,4,256]{2,1,0:T(4,128)S(1)}, f32[11,4,256]{2,1,0:T(4,128)S(1)}, u32[]{:S(2)}, u32[]{:S(2)}) collective-permute-start(f32[11,4,256]{2,1,0:T(4,128)S(1)} %pad_maximum_fusion.12), channel_id=1, source_target_pairs={{0,1},{1,2},{2,3},{3,4},{4,5},{5,6},{6,7},{7,8},{8,9},{9,10},{10,1... | collective-permute-start | bytes 135176 | tf_op jit(solution)/shard_map/ppermute | solution.py:29
where the time goes:
time: 113 us; the launch traced here: 112 us
  starting transfers between devices  35.2 us (31%)
  local copies, waits for them, and re-layouts  27 us (24%)
  blocking collectives  21.1 us (19%)
  waiting for transfers between devices  13.3 us (12%)
  other arithmetic  8.96 us (8%)
  matrix products  5.12 us (5%)
  between operations  1.4 us (1%)
    ppermute x3, starting transfers between devices, padded_2(): lax.ppermute(head, axis, [((i + 1) % count, i) for i in range(count)])  29.3 us
    all_to_all x1, blocking collectives, from_everyone(): return lax.all_to_all(copies, axis, split_axis=0, concat_axis=0, tiled=True)  21.1 us
    ppermute x3, waiting for transfers between devices, padded_2(): lax.ppermute(tail, axis, [(i, (i + 1) % count) for i in range(count)])  11.7 us
    unnamed x39, local copies, waits for them, and re-layouts  6.21 us
    ppermute x3, starting transfers between devices, padded_2(): lax.ppermute(tail, axis, [(i, (i + 1) % count) for i in range(count)])  5.94 us
    dot_general x2, matrix products, lift(): jnp.dot(spread_rows, fields.reshape(moment_count, -1), precision=lax.Prec...  4.72 us
    slice x4, local copies, waits for them, and re-layouts, upwind_sweep(): jnp.roll(cube_view, -1, 2)  3.25 us
    concatenate x2, local copies, waits for them, and re-layouts, upwind_sweep(): jnp.roll(cube_view, 1, 2)  2.52 us
  transfers between devices with their start and end apart: 6, of which 3 were waited for; matrix products, arithmetic and copies ran while one was open for 2% of the time, Pallas kernels for 0%

commit v1 on v0

v1 whole, which is shorter than its diff:
```python
import math

import jax
import jax.numpy as jnp
from jax import lax
from jax.experimental import pallas as pl
from jax.experimental.pallas import tpu as pltpu
from jax.sharding import PartitionSpec as P

F = jnp.float32
SHAPE = (8, 128)
VOL = 216.0 / 2304 / math.pi**1.5
K1, K4, K5 = 2.0, 0.6667, 0.8


def magnitude(kk):
    return 2.75 - 0.5 * kk


def iotas():
    return lax.broadcasted_iota(jnp.int32, SHAPE, 0), lax.broadcasted_iota(jnp.int32, SHAPE, 1)


def first_speed(i_ref):
    return jnp.full(SHAPE, -3.0 + (i_ref[0].astype(F) + 0.5) * 0.375, F)


def field_polynomial(a, m):
    a2 = a * a
    u, w = a2 - 1.5, a2 - 2.5
    return (
        m[0] + K1 * (a * m[1]) + K4 * (u * m[4]) + K5 * (a * w * m[5]),
        K1 * m[2] + K5 * (w * m[6]) + K1 * (a * m[8]),
        K1 * m[3] + K5 * (w * m[7]),
        K4 * m[4] + K5 * (a * m[5]),
        K5 * m[6],
        K5 * m[7],
        K1 * m[9],
    )


def at_second(al, b):
    b2 = b * b
    return (
        al[0] + b * al[1] + b2 * al[3] + (b2 * b) * al[4],
        al[2] + b2 * al[5] + b * al[6],
        al[3] + b * al[4],
        al[5],
    )


def from_z(h, lane, positive):
    inside = lane & 15
    if positive:
        return jnp.where(inside == 0, pltpu.roll(h, 113, 1), pltpu.roll(h, 1, 1))
    return jnp.where(inside == 15, pltpu.roll(h, 15, 1), pltpu.roll(h, 127, 1))


def from_y(h, lane, positive, swap):
    r = pltpu.roll(h, 16 if positive else 112, 1)
    return jnp.where(lane < 16 if positive else lane >= 112, swap(r), r)


def swap_halves(r):
    return pltpu.roll(r, 4, 0)


def swap_pairs(r):
    even = (lax.broadcasted_iota(jnp.int32, SHAPE, 0) & 1) == 0
    return jnp.where(even, pltpu.roll(r, 7, 0), pltpu.roll(r, 1, 0))


def add_raw(sums, b, acc):
    s0, sb, sc, s2, sb2, sc2, sbc = sums
    p, q, r, t = acc
    b2 = b * b
    return (
        s0 + p,
        sb + b * p,
        sc + q,
        s2 + b2 * p + r,
        sb2 + b * (b2 * p + r),
        sc2 + b2 * q + t,
        sbc + b * q,
    )


def pack_kernel(i_ref, x_ref, m_ref, p_ref, o_ref):
    def take(near, far):
        o_ref[0:288, :] = x_ref[pl.ds(near, 288, stride=4), :]
        o_ref[288:576, :] = x_ref[pl.ds(far, 288, stride=4), :]
        o_ref[576:596, :] = m_ref[pl.ds(near, 20, stride=4), :]
        o_ref[596:598, :] = p_ref[pl.ds(near, 2, stride=4), :].astype(F)
        o_ref[598:600, :] = jnp.zeros((2, 128), F)

    pl.when(i_ref[0] >= 8)(lambda: take(3, 2))
    pl.when(i_ref[0] < 8)(lambda: take(0, 1))


def local_kernel(i_ref, x_ref, m_ref, p_ref, h_ref, s_ref):
    a = first_speed(i_ref)
    aa = jnp.abs(a)
    sub, lane = iotas()
    pore = p_ref[...].astype(F)
    al = field_polynomial(a, [m_ref[m] for m in range(10)])
    zero = jnp.zeros(SHAPE, F)

    def sweeps(shift, edge):
        inner = jnp.where((sub & 3) == edge, 0.0, 1.0)

        def step(jj, sums):
            bm = 2.75 - 0.5 * jj.astype(F)
            ex = jnp.exp(-(a * a) - bm * bm)
            accs = [[zero] * 4, [zero] * 4]
            polys = [at_second(al, -bm), at_second(al, bm)]
            rows = [jj * 12, (11 - jj) * 12]
            for kk in range(6):
                cm = magnitude(kk)
                c2 = cm * cm
                pr = pore * (1.0 / (aa + (1.0 + cm + bm)))
                pg = pr * (ex * math.exp(-c2))
                px, py, pz = aa * pr * inner, bm * pr, cm * pr
                for side in range(2):
                    p0, p1, p2, p3 = polys[side]
                    even, odd = p0 + c2 * p2, cm * (p1 + c2 * p3)
                    out = []
                    for up in range(2):
                        v = rows[side] + (11 - kk if up else kk)
                        g = pg * (even + odd if up else even - odd)
                        h = x_ref[v]
                        for _ in range(2):
                            h = (
                                g
                                + px * pltpu.roll(h, shift, 0)
                                + py * from_y(h, lane, side == 1, swap_halves)
                                + pz * from_z(h, lane, up == 1)
                            )
                        h_ref[v] = h
                        out.append(h)
                    s, d = out[1] + out[0], cm * (out[1] - out[0])
                    p, q, r, t = accs[side]
                    accs[side] = [p + s, q + d, r + c2 * s, t + c2 * d]
            sums = add_raw(sums, -bm, accs[0])
            return add_raw(sums, bm, accs[1])

        sums = lax.fori_loop(0, 6, step, (zero,) * 7)
        for n in range(7):
            s_ref[n] = sums[n]

    pl.when(i_ref[0] >= 8)(lambda: sweeps(1, 0))
    pl.when(i_ref[0] < 8)(lambda: sweeps(7, 3))


def halo_kernel(i_ref, g_ref, p_ref, s_ref, o_ref, d_ref):
    a = first_speed(i_ref)
    aa = jnp.abs(a)
    sub, lane = iotas()
    even_row = (sub & 1) == 0
    zero = jnp.zeros(SHAPE, F)
    forward = i_ref[0] >= 8

    def row(ref, r):
        return jnp.broadcast_to(ref[r : r + 1, :].astype(F), SHAPE)

    def pair(ref, r, s):
        return jnp.where(even_row, row(ref, r), row(ref, s))

    def own(plus, minus):
        return jnp.where(forward, pair(p_ref, plus, plus + 4), pair(p_ref, minus, minus + 4))

    pore_out, pore_0, pore_1 = pair(g_ref, 596, 597), own(0, 3), own(1, 2)
    al = field_polynomial(a, [pair(g_ref, 576 + 2 * m, 577 + 2 * m) for m in range(10)])
    cs = [-2.75 + 0.5 * (4 * t + (sub >> 1)).astype(F) for t in range(3)]
    ecs = [jnp.exp(-c * c) for c in cs]

    def back(h, t):
        if t == 0:
            return from_z(h, lane, False)
        if t == 2:
            return from_z(h, lane, True)
        return jnp.where(sub < 4, from_z(h, lane, False), from_z(h, lane, True))

    def step(jj, carry):
        bm = 2.75 - 0.5 * jj.astype(F)
        ex = jnp.exp(-(a * a) - bm * bm)
        accs = [[[zero] * 4, [zero] * 4], [[zero] * 4, [zero] * 4]]
        polys = [at_second(al, -bm), at_second(al, bm)]
        rows = [jj * 24, (11 - jj) * 24]
        for t in range(3):
            c = cs[t]
            ca = jnp.abs(c)
            r = 1.0 / (aa + ca + (1.0 + bm))
            wa, wb, wc = aa * r, bm * r, ca * r
            rg = r * ex * ecs[t]
            for side in range(2):
                p0, p1, p2, p3 = polys[side]
                g = rg * (p0 + c * (p1 + c * (p2 + c * p3)))
                base = pl.multiple_of(rows[side] + 8 * t, 8)
                near, far = g_ref[pl.ds(base, 8), :], g_ref[pl.ds(288 + base, 8), :]
                outer = pore_out * (
                    g + wa * far + wb * from_y(near, lane, side == 1, swap_pairs) + wc * back(near, t)
                )
                first = pore_0 * wa * near
                e0 = pore_0 * (
                    wa * outer + wb * from_y(first, lane, side == 1, swap_pairs) + wc * back(first, t)
                )
                e1 = pore_1 * wa * first
                d_ref[pl.ds(base, 8), :] = e0
                d_ref[pl.ds(288 + base, 8), :] = e1
                for n, e in enumerate((e0, e1)):
                    p, q, u, w = accs[n][side]
                    ce = c * e
                    cce = c * ce
                    accs[n][side] = [p + e, q + ce, u + cce, w + c * cce]
        return tuple(
            add_raw(add_raw(carry[n], -bm, accs[n][0]), bm, accs[n][1]) for n in range(2)
        )

    near_sums, far_sums = lax.fori_loop(0, 6, step, ((zero,) * 7, (zero,) * 7))
    place = sub & 3
    at_near = place == jnp.where(forward, 0, 3)
    at_far = place == jnp.where(forward, 1, 2)
    straight = (sub < 4) == even_row

    def spread(x):
        x = x + pltpu.roll(x, 2, 0)
        x = x + pltpu.roll(x, 4, 0)
        return jnp.where(straight, x, pltpu.roll(x, 1, 0))

    s = [
        s_ref[n] + jnp.where(at_near, spread(near_sums[n]), jnp.where(at_far, spread(far_sums[n]), 0.0))
        for n in range(7)
    ]
    s0, sb, sc, s2, sb2, sc2, sbc = s
    a2 = a * a
    t4, t5 = (a2 - 1.5) * s0 + s2, (a2 - 2.5) * s0 + s2
    moments = (s0, a * s0, sb, sc, t4, a * t5, (a2 - 2.5) * sb + sb2, (a2 - 2.5) * sc + sc2, a * sb, sbc)
    for m in range(10):
        value = moments[m] * VOL
        for n in range(o_ref.shape[0]):
            o_ref[n, m] = value


def final_kernel(i_ref, r_ref, h_ref, d_ref, p_ref, c_ref, left_ref, right_ref, mh_ref, o_ref, mo_ref, k_ref):
    a = first_speed(i_ref)
    sub, lane = iotas()
    pores = [left_ref[10], p_ref[...].astype(F), right_ref[10]]
    low, high = (sub & 3) == 0, (sub & 3) == 3

    def around(h):
        up = pltpu.roll(h, 16, 1)
        down = pltpu.roll(h, 112, 1)
        return (
            jnp.where(lane < 16, swap_halves(up), up)
            + jnp.where(lane >= 112, swap_halves(down), down)
            + from_z(h, lane, True)
            + from_z(h, lane, False)
        )

    for m in range(10):
        inv = 1.0 / (jnp.full(SHAPE, r_ref[m], F) + 6.0)
        q = [p * inv for p in pores]
        change = [left_ref[m], c_ref[m], right_ref[m]]
        cor = [q[n] * change[n] for n in range(3)]
        for it in range(4):
            new = list(cor)
            for n in range(3):
                if it == 3 and n != 1:
                    continue
                below = pltpu.roll(cor[n], 1, 0)
                above = pltpu.roll(cor[n], 7, 0)
                if n > 0:
                    below = jnp.where(low, pltpu.roll(cor[n - 1], 5, 0), below)
                if n < 2:
                    above = jnp.where(high, pltpu.roll(cor[n + 1], 3, 0), above)
                new[n] = q[n] * (change[n] + (below + above + around(cor[n])))
            cor = new
        k_ref[m] = cor[1]
        mo_ref[m] = mh_ref[m] + cor[1]

    al = field_polynomial(a, [k_ref[m] for m in range(10)])
    pore = pores[1]

    def step(jj, carry):
        bm = 2.75 - 0.5 * jj.astype(F)
        ex = pore * jnp.exp(-(a * a) - bm * bm)
        for side in range(2):
            p0, p1, p2, p3 = at_second(al, bm if side else -bm)
            base = (11 - jj if side else jj) * 12
            for kk in range(6):
                cm = magnitude(kk)
                c2 = cm * cm
                w = ex * math.exp(-c2)
                even, odd = w * (p0 + c2 * p2), w * (cm * (p1 + c2 * p3))
                for up in range(2):
                    v = base + (11 - kk if up else kk)
                    o_ref[pl.ds(v * 8, 8), :] = h_ref[v] + (even + odd if up else even - odd)
        return carry

    lax.fori_loop(0, 6, step, 0)

    def put(near, far):
        o_ref[pl.ds(near, 288, stride=4), :] = o_ref[pl.ds(near, 288, stride=4), :] + d_ref[0:288, :]
        o_ref[pl.ds(far, 288, stride=4), :] = o_ref[pl.ds(far, 288, stride=4), :] + d_ref[288:576, :]

    pl.when(i_ref[0] >= 8)(lambda: put(0, 1))
    pl.when(i_ref[0] < 8)(lambda: put(3, 2))


def call(kernel, outs, smem, vmem, cost, scratch=()):
    vm = pl.BlockSpec(memory_space=pltpu.VMEM)
    sm = pl.BlockSpec(memory_space=pltpu.SMEM)
    shapes = [jax.ShapeDtypeStruct(s, F) for s in outs]
    return pl.pallas_call(
        kernel,
        out_shape=shapes if len(shapes) > 1 else shapes[0],
        in_specs=[sm] * len(smem) + [vm] * len(vmem),
        out_specs=[vm] * len(shapes) if len(shapes) > 1 else vm,
        scratch_shapes=list(scratch),
        cost_estimate=pl.CostEstimate(flops=cost, bytes_accessed=4 * cost, transcendentals=0),
    )(*smem, *vmem)


def to_registers(x):
    n = x.shape[0]
    return x.reshape(n, 4, 2, 128).transpose(0, 2, 1, 3).reshape(n, 8, 128)


def from_registers(x):
    n = x.shape[0]
    return x.reshape(n, 2, 4, 128).transpose(0, 2, 1, 3).reshape(n, 4, 256)


def groups_of(key):
    found = {}
    for v in range(16):
        found.setdefault(key(v), []).append(v)
    return list(found.values())


FAR = groups_of(lambda v: (v // 8, v % 2))
NEAR = groups_of(lambda v: (v % 8) // 2)


def upwind_pairs(space):
    return [
        (v * space + s, v * space + (s + (1 if v >= 8 else -1)) % space) for v in range(16) for s in range(space)
    ]


def body(distribution, moments_old, pore_mask, synthetic_rate):
    space = lax.axis_size("space")
    i = lax.axis_index("vel").astype(jnp.int32).reshape(1)
    x = to_registers(distribution)
    old = to_registers(moments_old)
    pore = to_registers(pore_mask[None])[0]
    packed = call(
        pack_kernel, [(600, 128)], [i], [x.reshape(1152, 128), old.reshape(80, 128), pore], 1 << 16
    )
    halo = lax.ppermute(packed, ("vel", "space"), upwind_pairs(space))
    half, sums = call(local_kernel, [(144, 8, 128), (7, 8, 128)], [i], [x, old, pore], 1 << 23)
    copies, extra = call(halo_kernel, [(4, 10, 8, 128), (576, 128)], [i], [halo, pore, sums], 1 << 18)
    got = lax.all_to_all(
        copies.reshape(4, 80, 128), "vel", 0, 0, axis_index_groups=FAR, tiled=True
    )
    total = jnp.sum(got, axis=0)
    got = lax.all_to_all(
        jnp.broadcast_to(total, (4, 80, 128)), "vel", 0, 0, axis_index_groups=NEAR, tiled=True
    )
    moments_half = jnp.sum(got, axis=0)
    change = moments_half - old.reshape(80, 128)
    message = jnp.concatenate([change, pore.astype(F)], axis=0)
    count = [(s, (s + 1) % space) for s in range(space)]
    left = lax.ppermute(message, "space", count)
    right = lax.ppermute(message, "space", [(t, s) for s, t in count])
    out, moments_new = call(
        final_kernel,
        [(1152, 128), (10, 8, 128)],
        [i, synthetic_rate],
        [
            half,
            extra,
            pore,
            change.reshape(10, 8, 128),
            left.reshape(11, 8, 128),
            right.reshape(11, 8, 128),
            moments_half.reshape(10, 8, 128),
        ],
        1 << 20,
        [pltpu.VMEM((10, 8, 128), F)],
    )
    return from_registers(out.reshape(144, 8, 128)), from_registers(moments_new)


def solution(mesh):
    placed = (P("vel", "space", None), P(None, "space", None), P("space", None), P())
    return jax.shard_map(
        body,
        mesh=mesh,
        in_specs=placed,
        out_specs=(P("vel", "space", None), P(None, "space", None)),
        check_vma=False,
    )
```

time: 113 us -> 75.7 us (0.67)
  local copies, waits for them, and re-layouts: 27 us -> 2.01 us
  Pallas kernels: 0 us -> 12.3 us
  other arithmetic: 8.96 us -> 0.66 us
  blocking collectives: 21.1 us -> 15.3 us
  matrix products: 5.12 us -> 0 us
  starting transfers between devices: 35.2 us -> 32.4 us
  waiting for transfers between devices: 13.3 us -> 11.9 us
    pallas_call x0 -> x4, Pallas kernels: none -> 12.3 us  [call(): pl.pallas_call(kernel, out_shape=shapes if len(shapes) > 1 else shapes[0]...]
    concatenate x8 -> x0, local copies, waits for them, and re-layouts: 9.99 us -> none  [the longest x2 2.52 us: upwind_sweep(): jnp.roll(cube_view, 1, 2)]
    ppermute x6 -> x3, starting transfers between devices: 35.2 us -> 28 us  [the longest x1 21.1 us: body(): halo = lax.ppermute(packed, ('vel', 'space'), upwind_pairs(space))]
    slice x32 -> x0, local copies, waits for them, and re-layouts: 6.85 us -> none  [the longest x4 3.25 us: upwind_sweep(): jnp.roll(cube_view, -1, 2)]
    all_to_all x1, blocking collectives: 21.1 us -> 15.3 us  [body(): lax.all_to_all(copies.reshape(4, 80, 128), 'vel', 0, 0, axis_index_groups...]
    ppermute x6 -> x3, waiting for transfers between devices: 13.3 us -> 7.8 us  [the longest x1 7.03 us: body(): left = lax.ppermute(message, 'space', count)]
    dot_general x3 -> x0, matrix products: 5.12 us -> none  [the longest x2 4.72 us: lift(): jnp.dot(spread_rows, fields.reshape(moment_count, -1), precision=lax.Prec...]
    unnamed x39 -> x12, local copies, waits for them, and re-layouts: 6.21 us -> 1.33 us
  transfers between devices with their start and end apart: 6 -> 4, of which waited for: 3 -> 3; matrix products, arithmetic and copies ran while one was open for 2% -> 1% of each run, Pallas kernels for 0% -> 5%
where the time goes in v1:
time: 75.7 us; the launch traced here: 75.2 us
  starting transfers between devices  32.4 us (43%)
  blocking collectives  15.3 us (20%)
  Pallas kernels  12.3 us (16%)
  waiting for transfers between devices  11.9 us (16%)
  local copies, waits for them, and re-layouts  2.01 us (3%)
    ppermute x1, starting transfers between devices, body(): halo = lax.ppermute(packed, ('vel', 'space'), upwind_pairs(space))  21.1 us
    all_to_all x1, blocking collectives, body(): lax.all_to_all(copies.reshape(4, 80, 128), 'vel', 0, 0, axis_index_groups...  15.3 us
    pallas_call x4, Pallas kernels, call(): pl.pallas_call(kernel, out_shape=shapes if len(shapes) > 1 else shapes[0]...  12.3 us
    ppermute x1, waiting for transfers between devices, body(): left = lax.ppermute(message, 'space', count)  7.03 us
    ppermute x1, starting transfers between devices, body(): right = lax.ppermute(message, 'space', [(t, s) for s, t in count])  4.92 us
    all_to_all x1, starting transfers between devices, body(): lax.all_to_all(jnp.broadcast_to(total, (4, 80, 128)), 'vel', 0, 0, axis_i...  4.44 us
    all_to_all x1, waiting for transfers between devices, body(): lax.all_to_all(jnp.broadcast_to(total, (4, 80, 128)), 'vel', 0, 0, axis_i...  4.08 us
    ppermute x1, starting transfers between devices, body(): left = lax.ppermute(message, 'space', count)  1.92 us
  transfers between devices with their start and end apart: 4, of which 3 were waited for; matrix products, arithmetic and copies ran while one was open for 1% of the time, Pallas kernels for 5%

profile of v1, /device:TPU:2, one launch (start us, length us, event | category | flops | bytes accessed | tf_op | source)
XLA Modules:
  0.0 75.2 jit_solution(5463705861736370682)
XLA Ops:
  0.6 1.8 %shard_map.60 = f32[600,128]{1,0:T(8,128)} custom-call(s32[1]{0:T(128)} %bitcast.i_ref, f32[1152,128]{1,0:T(8,128)} %bitcast.35, f32[80,128]{1,0:T(8,128)} %bitcast.37, s32[8,128]{1,0:T(8,128)} %bitcast.43), custom_call_target="tpu_custom_call" | custom-call | flops 65536 | bytes 262144 | tf_op jit(solution)/shard_map/pallas_call | solution.py:314
  2.5 21.1 %collective-permute-start = (f32[600,128]{1,0:T(8,128)}, f32[600,128]{1,0:T(8,128)S(1)}, u32[]{:S(2)}, u32[]{:S(2)}) collective-permute-start(f32[600,128]{1,0:T(8,128)} %shard_map.60), channel_id=1, source_target_pairs={{0,63},{1,0},{2,1},{3,2},{4,3},{5,4},{6,5},{7,6},{8,7},{9,8},{10,9... | collective-permute-start | bytes 921608 | tf_op jit(solution)/shard_map/ppermute | solution.py:360
  23.6 3.9 %shard_map.59 = (f32[144,8,128]{2,1,0:T(8,128)}, f32[7,8,128]{2,1,0:T(8,128)}) custom-call(s32[1]{0:T(128)} %bitcast.i_ref, f32[144,8,128]{2,1,0:T(8,128)} %bitcast.36, f32[10,8,128]{2,1,0:T(8,128)} %bitcast.38, s32[8,128]{1,0:T(8,128)} %bitcast.44), custom_call_target="tpu_custom_call" | custom-call | flops 8388608 | bytes 33554432 | tf_op jit(solution)/shard_map/pallas_call | solution.py:314
  27.5 0.8 %collective-permute-done.g_ref = f32[600,128]{1,0:T(8,128)S(1)} collective-permute-done((f32[600,128]{1,0:T(8,128)}, f32[600,128]{1,0:T(8,128)S(1)}, u32[]{:S(2)}, u32[]{:S(2)}) %collective-permute-start) | collective-permute-done | bytes 307232 | tf_op jit(solution)/shard_map/ppermute | solution.py:360
  28.3 0.0 copy-start.2
  28.3 0.7 copy-done.2
  29.0 2.5 %shard_map.61 = (f32[4,10,8,128]{3,2,1,0:T(8,128)}, f32[576,128]{1,0:T(8,128)}) custom-call(s32[1]{0:T(128)} %bitcast.i_ref, f32[600,128]{1,0:T(8,128)} %copy-done.2, s32[8,128]{1,0:T(8,128)} %bitcast.45, f32[7,8,128]{2,1,0:T(8,128)} %get-tuple-element.9.s_ref), custom_call_target="tpu_custom_call" | custom-call | flops 262144 | bytes 1048576 | tf_op jit(solution)/shard_map/pallas_call | solution.py:314
  31.5 15.3 %all_to_all.10 = f32[4,80,128]{2,1,0:T(8,128)S(1)} all-to-all(f32[4,80,128]{2,1,0:T(8,128)} %bitcast.42), channel_id=1, replica_groups={{0,128,256,384},{64,192,320,448},{512,640,768,896},{576,704,832,960},{1..., dimensions={0} | all-to-all | bytes 327680 | tf_op jit(solution)/shard_map/all_to_all | solution.py:363
  46.8 0.7 broadcast_in_dim.3
  47.5 0.0 copy-start.3
  47.5 4.4 %all-to-all-start.1 = ((f32[4,80,128]{2,1,0:T(8,128)}), f32[4,80,128]{2,1,0:T(8,128)S(1)}, u32[]{:S(2)}, u32[]{:S(2)}) async-start(f32[4,80,128]{2,1,0:T(8,128)} %broadcast_in_dim.3), calls=%async_computation.1 | async-start | bytes 327680 | tf_op jit(solution)/shard_map/all_to_all | solution.py:367
  51.9 0.0 copy-done.3
  52.0 4.1 %all-to-all-done.1 = f32[4,80,128]{2,1,0:T(8,128)S(1)} async-done(((f32[4,80,128]{2,1,0:T(8,128)}), f32[4,80,128]{2,1,0:T(8,128)S(1)}, u32[]{:S(2)}, u32[]{:S(2)}) %all-to-all-start.1) | async-done | bytes 163872 | tf_op jit(solution)/shard_map/all_to_all | solution.py:367
  56.1 0.0 copy-done
  56.1 0.0 copy-start.1
  56.1 4.9 %collective-permute-start.2 = (f32[88,128]{1,0:T(8,128)S(1)}, f32[88,128]{1,0:T(8,128)S(1)}, u32[]{:S(2)}, u32[]{:S(2)}) collective-permute-start(f32[88,128]{1,0:T(8,128)S(1)} %pad_maximum_fusion), channel_id=1, source_target_pairs={{1,0},{2,1},{3,2},{4,3},{5,4},{6,5},{7,6},{8,7},{9,8},{10,9},{11,1... | collective-permute-start | bytes 135176 | tf_op jit(solution)/shard_map/ppermute | solution.py:375
  61.0 1.9 %collective-permute-start.1 = (f32[88,128]{1,0:T(8,128)S(1)}, f32[88,128]{1,0:T(8,128)S(1)}, u32[]{:S(2)}, u32[]{:S(2)}) collective-permute-start(f32[88,128]{1,0:T(8,128)S(1)} %pad_maximum_fusion), channel_id=1, source_target_pairs={{0,1},{1,2},{2,3},{3,4},{4,5},{5,6},{6,7},{7,8},{8,9},{9,10},{10,1... | collective-permute-start | bytes 135176 | tf_op jit(solution)/shard_map/ppermute | solution.py:374
  63.0 0.0 copy-done.1
  63.0 0.6 bitcast_subtract_fusion.c_ref
  63.6 0.0 collective-permute-done.2
  63.6 7.0 %collective-permute-done.1 = f32[88,128]{1,0:T(8,128)S(1)} collective-permute-done((f32[88,128]{1,0:T(8,128)S(1)}, f32[88,128]{1,0:T(8,128)S(1)}, u32[]{:S(2)}, u32[]{:S(2)}) %collective-permute-start.1) | collective-permute-done | bytes 45088 | tf_op jit(solution)/shard_map/ppermute | solution.py:374
  70.6 0.0 copy-done.4
  70.6 0.6 copy-done.5
  71.2 4.0 %shard_map.62 = (f32[1152,128]{1,0:T(8,128)}, f32[10,8,128]{2,1,0:T(8,128)}) custom-call(s32[1]{0:T(128)} %bitcast.i_ref, f32[10]{0:T(128)} %r_ref.1, f32[144,8,128]{2,1,0:T(8,128)} %get-tuple-element.8.h_ref, f32[576,128]{1,0:T(8,128)} %get-tuple-element.10.d_ref, s32[8,128]{1,0:T(8,128)} %bitcast.46, f32[10,8,128]{2,1,0:T(8,128)} %bitcast_subtract_fusion.c_ref, ...), custom_call_target="tpu_custom_call" | custom-call | flops 1048576 | bytes 4194304 | tf_op jit(solution)/shard_map/pallas_call | solution.py:314
  (8 shorter events, 0.0 us)
Async XLA Ops:
  2.5 25.8 %collective-permute-start = (f32[600,128]{1,0:T(8,128)}, f32[600,128]{1,0:T(8,128)S(1)}, u32[]{:S(2)}, u32[]{:S(2)}) collective-permute-start(f32[600,128]{1,0:T(8,128)} %shard_map.60), channel_id=1, source_target_pairs={{0,63},{1,0},{2,1},{3,2},{4,3},{5,4},{6,5},{7,6},{8,7},{9,8},{10,9... | collective-permute-start | bytes 921608 | tf_op jit(solution)/shard_map/ppermute | solution.py:360
  28.3 0.7 copy-start.2
  47.5 4.4 %copy-start.3 = (s32[4,256]{1,0:T(4,128)S(1)}, s32[4,256]{1,0:T(4,128)}, u32[]{:S(2)}) copy-start(s32[4,256]{1,0:T(4,128)} %param.6) | copy-start | bytes 12292
  47.5 8.5 %all-to-all-start.1 = ((f32[4,80,128]{2,1,0:T(8,128)}), f32[4,80,128]{2,1,0:T(8,128)S(1)}, u32[]{:S(2)}, u32[]{:S(2)}) async-start(f32[4,80,128]{2,1,0:T(8,128)} %broadcast_in_dim.3), calls=%async_computation.1 | async-start | bytes 327680 | tf_op jit(solution)/shard_map/all_to_all | solution.py:367
  52.0 4.1 %copy-start = (f32[10,4,256]{2,1,0:T(4,128)S(1)}, f32[10,4,256]{2,1,0:T(4,128)}, u32[]{:S(2)}) copy-start(f32[10,4,256]{2,1,0:T(4,128)} %param.5) | copy-start | bytes 122884
  56.1 6.9 %copy-start.1 = (f32[80,128]{1,0:T(8,128)}, f32[80,128]{1,0:T(8,128)S(1)}, u32[]{:S(2)}) copy-start(f32[80,128]{1,0:T(8,128)S(1)} %reduce_sum.21) | copy-start | bytes 122884
  56.1 7.5 %collective-permute-start.2 = (f32[88,128]{1,0:T(8,128)S(1)}, f32[88,128]{1,0:T(8,128)S(1)}, u32[]{:S(2)}, u32[]{:S(2)}) collective-permute-start(f32[88,128]{1,0:T(8,128)S(1)} %pad_maximum_fusion), channel_id=1, source_target_pairs={{1,0},{2,1},{3,2},{4,3},{5,4},{6,5},{7,6},{8,7},{9,8},{10,9},{11,1... | collective-permute-start | bytes 135176 | tf_op jit(solution)/shard_map/ppermute | solution.py:375
  61.0 9.6 %collective-permute-start.1 = (f32[88,128]{1,0:T(8,128)S(1)}, f32[88,128]{1,0:T(8,128)S(1)}, u32[]{:S(2)}, u32[]{:S(2)}) collective-permute-start(f32[88,128]{1,0:T(8,128)S(1)} %pad_maximum_fusion), channel_id=1, source_target_pairs={{0,1},{1,2},{2,3},{3,4},{4,5},{5,6},{6,7},{7,8},{8,9},{9,10},{10,1... | collective-permute-start | bytes 135176 | tf_op jit(solution)/shard_map/ppermute | solution.py:374
  63.6 7.0 %copy-start.4 = (f32[88,128]{1,0:T(8,128)}, f32[88,128]{1,0:T(8,128)S(1)}, u32[]{:S(2)}) copy-start(f32[88,128]{1,0:T(8,128)S(1)} %collective-permute-done.2) | copy-start | bytes 135172
  70.6 0.6 copy-start.5

commit v2 on v1

--- a/solution.py
+++ b/solution.py
@@ -317,6 +317,7 @@
         in_specs=[sm] * len(smem) + [vm] * len(vmem),
         out_specs=[vm] * len(shapes) if len(shapes) > 1 else vm,
         scratch_shapes=list(scratch),
+        compiler_params=pltpu.CompilerParams(vmem_limit_bytes=4 << 20),
         cost_estimate=pl.CostEstimate(flops=cost, bytes_accessed=4 * cost, transcendentals=0),
     )(*smem, *vmem)
 

time: 75.7 us -> 72.8 us (0.962)
  Pallas kernels: 12.3 us -> 6.13 us
  waiting for transfers between devices: 11.9 us -> 14.1 us
  local copies, waits for them, and re-layouts: 2.01 us -> 3.86 us
    pallas_call x4, Pallas kernels: 12.3 us -> 6.13 us  [call(): pl.pallas_call(kernel, out_shape=shapes if len(shapes) > 1 else shapes[0]...]
    unnamed x12 -> x10, local copies, waits for them, and re-layouts: 1.33 us -> 3.18 us
    ppermute x1, waiting for transfers between devices: 0.77 us -> 2.35 us  [body(): halo = lax.ppermute(packed, ('vel', 'space'), upwind_pairs(space))]
  transfers between devices with their start and end apart: 4 -> 4, of which waited for: 3 -> 4; matrix products, arithmetic and copies ran while one was open for 1% -> 0% of each run, Pallas kernels for 5% -> 3%
where the time goes in v2:
time: 72.8 us; the launch traced here: 72.3 us
  starting transfers between devices  32.7 us (45%)
  blocking collectives  14.7 us (20%)
  waiting for transfers between devices  14.1 us (19%)
  Pallas kernels  6.13 us (8%)
  local copies, waits for them, and re-layouts  3.86 us (5%)
  between operations  0.73 us (1%)
    ppermute x1, starting transfers between devices, body(): halo = lax.ppermute(packed, ('vel', 'space'), upwind_pairs(space))  21.1 us
    all_to_all x1, blocking collectives, body(): lax.all_to_all(copies.reshape(4, 80, 128), 'vel', 0, 0, axis_index_groups...  14.7 us
    ppermute x1, waiting for transfers between devices, body(): left = lax.ppermute(message, 'space', count)  7.53 us
    pallas_call x4, Pallas kernels, call(): pl.pallas_call(kernel, out_shape=shapes if len(shapes) > 1 else shapes[0]...  6.13 us
    ppermute x1, starting transfers between devices, body(): right = lax.ppermute(message, 'space', [(t, s) for s, t in count])  5.03 us
    all_to_all x1, starting transfers between devices, body(): lax.all_to_all(jnp.broadcast_to(total, (4, 80, 128)), 'vel', 0, 0, axis_i...  4.65 us
    all_to_all x1, waiting for transfers between devices, body(): lax.all_to_all(jnp.broadcast_to(total, (4, 80, 128)), 'vel', 0, 0, axis_i...  4.09 us
    unnamed x10, local copies, waits for them, and re-layouts  3.18 us
  transfers between devices with their start and end apart: 4, of which 4 were waited for; matrix products, arithmetic and copies ran while one was open for 0% of the time, Pallas kernels for 3%

profile of v2, /device:TPU:2, one launch (start us, length us, event | category | flops | bytes accessed | tf_op | source)
XLA Modules:
  0.0 72.3 jit_solution(8134679813742161568)
XLA Ops:
  0.6 0.0 copy-start.3
  0.6 0.7 copy-done.3
  1.3 0.0 copy-start
  1.3 1.1 %copy-done = f32[144,4,256]{2,1,0:T(4,128)S(1)} copy-done((f32[144,4,256]{2,1,0:T(4,128)S(1)}, f32[144,4,256]{2,1,0:T(4,128)}, u32[]{:S(2)}) %copy-start) | copy-done | bytes 589848
  2.4 0.0 copy-start.1
  2.4 0.8 %copy-done.1 = f32[10,4,256]{2,1,0:T(4,128)S(1)} copy-done((f32[10,4,256]{2,1,0:T(4,128)S(1)}, f32[10,4,256]{2,1,0:T(4,128)}, u32[]{:S(2)}) %copy-start.1) | copy-done | bytes 40984
  3.2 21.1 %collective-permute-start = (f32[600,128]{1,0:T(8,128)S(1)}, f32[600,128]{1,0:T(8,128)S(1)}, u32[]{:S(2)}, u32[]{:S(2)}) collective-permute-start(f32[600,128]{1,0:T(8,128)S(1)} %shard_map.60), channel_id=1, source_target_pairs={{0,63},{1,0},{2,1},{3,2},{4,3},{5,4},{6,5},{7,6},{8,7},{9,8},{10,9... | collective-permute-start | bytes 921608 | tf_op jit(solution)/shard_map/ppermute | solution.py:361
  24.3 2.0 %shard_map.59 = (f32[144,8,128]{2,1,0:T(8,128)S(1)}, f32[7,8,128]{2,1,0:T(8,128)S(1)}) custom-call(s32[1]{0:T(128)} %bitcast.i_ref, f32[144,8,128]{2,1,0:T(8,128)S(1)} %bitcast.36, f32[10,8,128]{2,1,0:T(8,128)S(1)} %bitcast.38, s32[8,128]{1,0:T(8,128)S(1)} %bitcast.44), custom_call_target="tpu_custom_call" | custom-call | flops 8388608 | bytes 33554432 | tf_op jit(solution)/shard_map/pallas_call | solution.py:314
  26.3 2.4 %collective-permute-done.g_ref = f32[600,128]{1,0:T(8,128)S(1)} collective-permute-done((f32[600,128]{1,0:T(8,128)S(1)}, f32[600,128]{1,0:T(8,128)S(1)}, u32[]{:S(2)}, u32[]{:S(2)}) %collective-permute-start) | collective-permute-done | bytes 307232 | tf_op jit(solution)/shard_map/ppermute | solution.py:361
  28.7 0.8 %shard_map.61 = (f32[4,10,8,128]{3,2,1,0:T(8,128)S(1)}, f32[576,128]{1,0:T(8,128)S(1)}) custom-call(s32[1]{0:T(128)} %bitcast.i_ref, f32[600,128]{1,0:T(8,128)S(1)} %collective-permute-done.g_ref, s32[8,128]{1,0:T(8,128)S(1)} %bitcast.45, f32[7,8,128]{2,1,0:T(8,128)S(1)} %get-tuple-element.9.s_ref), custom_call_target="tpu_custom_call" | custom-call | flops 262144 | bytes 1048576 | tf_op jit(solution)/shard_map/pallas_call | solution.py:314
  29.5 14.7 %all_to_all.10 = f32[4,80,128]{2,1,0:T(8,128)S(1)} all-to-all(f32[4,80,128]{2,1,0:T(8,128)S(1)} %bitcast.42), channel_id=1, replica_groups={{0,128,256,384},{64,192,320,448},{512,640,768,896},{576,704,832,960},{1..., dimensions={0} | all-to-all | bytes 327680 | tf_op jit(solution)/shard_map/all_to_all | solution.py:364
  44.3 0.7 broadcast_in_dim.3
  44.9 4.7 %all-to-all-start.1 = ((f32[4,80,128]{2,1,0:T(8,128)}), f32[4,80,128]{2,1,0:T(8,128)S(1)}, u32[]{:S(2)}, u32[]{:S(2)}) async-start(f32[4,80,128]{2,1,0:T(8,128)} %broadcast_in_dim.3), calls=%async_computation.1 | async-start | bytes 327680 | tf_op jit(solution)/shard_map/all_to_all | solution.py:368
  49.6 0.0 copy-start.2
  49.6 4.1 %all-to-all-done.1 = f32[4,80,128]{2,1,0:T(8,128)S(1)} async-done(((f32[4,80,128]{2,1,0:T(8,128)}), f32[4,80,128]{2,1,0:T(8,128)S(1)}, u32[]{:S(2)}, u32[]{:S(2)}) %all-to-all-start.1) | async-done | bytes 163872 | tf_op jit(solution)/shard_map/all_to_all | solution.py:368
  53.7 0.0 copy-done.2
  53.7 5.0 %collective-permute-start.2 = (f32[88,128]{1,0:T(8,128)S(1)}, f32[88,128]{1,0:T(8,128)S(1)}, u32[]{:S(2)}, u32[]{:S(2)}) collective-permute-start(f32[88,128]{1,0:T(8,128)S(1)} %pad_maximum_fusion), channel_id=1, source_target_pairs={{1,0},{2,1},{3,2},{4,3},{5,4},{6,5},{7,6},{8,7},{9,8},{10,9},{11,1... | collective-permute-start | bytes 135176 | tf_op jit(solution)/shard_map/ppermute | solution.py:376
  58.8 1.9 %collective-permute-start.1 = (f32[88,128]{1,0:T(8,128)S(1)}, f32[88,128]{1,0:T(8,128)S(1)}, u32[]{:S(2)}, u32[]{:S(2)}) collective-permute-start(f32[88,128]{1,0:T(8,128)S(1)} %pad_maximum_fusion), channel_id=1, source_target_pairs={{0,1},{1,2},{2,3},{3,4},{4,5},{5,6},{6,7},{7,8},{8,9},{9,10},{10,1... | collective-permute-start | bytes 135176 | tf_op jit(solution)/shard_map/ppermute | solution.py:375
  60.7 0.1 collective-permute-done.2
  60.8 7.5 %collective-permute-done.1 = f32[88,128]{1,0:T(8,128)S(1)} collective-permute-done((f32[88,128]{1,0:T(8,128)S(1)}, f32[88,128]{1,0:T(8,128)S(1)}, u32[]{:S(2)}, u32[]{:S(2)}) %collective-permute-start.1) | collective-permute-done | bytes 45088 | tf_op jit(solution)/shard_map/ppermute | solution.py:375
  68.4 0.0 copy-start.4
  68.4 0.7 copy-done.4
  69.0 3.3 %shard_map.62 = (f32[1152,128]{1,0:T(8,128)}, f32[10,8,128]{2,1,0:T(8,128)}) custom-call(s32[1]{0:T(128)} %bitcast.i_ref, f32[10]{0:T(128)S(1)} %copy-done.4, f32[144,8,128]{2,1,0:T(8,128)S(1)} %get-tuple-element.8.h_ref, f32[576,128]{1,0:T(8,128)S(1)} %get-tuple-element.10.d_ref, s32[8,128]{1,0:T(8,128)S(1)} %bitcast.47, ...), custom_call_target="tpu_custom_call" | custom-call | flops 1048576 | bytes 4194304 | tf_op jit(solution)/shard_map/pallas_call | solution.py:314
  (7 shorter events, 0.1 us)
Async XLA Ops:
  0.6 0.7 copy-start.3
  1.3 1.1 %copy-start = (f32[144,4,256]{2,1,0:T(4,128)S(1)}, f32[144,4,256]{2,1,0:T(4,128)}, u32[]{:S(2)}) copy-start(f32[144,4,256]{2,1,0:T(4,128)} %param.4) | copy-start | bytes 1769476
  2.4 0.8 %copy-start.1 = (f32[10,4,256]{2,1,0:T(4,128)S(1)}, f32[10,4,256]{2,1,0:T(4,128)}, u32[]{:S(2)}) copy-start(f32[10,4,256]{2,1,0:T(4,128)} %param.5) | copy-start | bytes 122884
  3.2 25.5 %collective-permute-start = (f32[600,128]{1,0:T(8,128)S(1)}, f32[600,128]{1,0:T(8,128)S(1)}, u32[]{:S(2)}, u32[]{:S(2)}) collective-permute-start(f32[600,128]{1,0:T(8,128)S(1)} %shard_map.60), channel_id=1, source_target_pairs={{0,63},{1,0},{2,1},{3,2},{4,3},{5,4},{6,5},{7,6},{8,7},{9,8},{10,9... | collective-permute-start | bytes 921608 | tf_op jit(solution)/shard_map/ppermute | solution.py:361
  44.9 8.7 %all-to-all-start.1 = ((f32[4,80,128]{2,1,0:T(8,128)}), f32[4,80,128]{2,1,0:T(8,128)S(1)}, u32[]{:S(2)}, u32[]{:S(2)}) async-start(f32[4,80,128]{2,1,0:T(8,128)} %broadcast_in_dim.3), calls=%async_computation.1 | async-start | bytes 327680 | tf_op jit(solution)/shard_map/all_to_all | solution.py:368
  49.6 4.1 %copy-start.2 = (f32[10,4,256]{2,1,0:T(4,128)S(1)}, f32[10,4,256]{2,1,0:T(4,128)}, u32[]{:S(2)}) copy-start(f32[10,4,256]{2,1,0:T(4,128)} %param.5) | copy-start | bytes 122884
  53.7 7.1 %collective-permute-start.2 = (f32[88,128]{1,0:T(8,128)S(1)}, f32[88,128]{1,0:T(8,128)S(1)}, u32[]{:S(2)}, u32[]{:S(2)}) collective-permute-start(f32[88,128]{1,0:T(8,128)S(1)} %pad_maximum_fusion), channel_id=1, source_target_pairs={{1,0},{2,1},{3,2},{4,3},{5,4},{6,5},{7,6},{8,7},{9,8},{10,9},{11,1... | collective-permute-start | bytes 135176 | tf_op jit(solution)/shard_map/ppermute | solution.py:376
  58.8 9.6 %collective-permute-start.1 = (f32[88,128]{1,0:T(8,128)S(1)}, f32[88,128]{1,0:T(8,128)S(1)}, u32[]{:S(2)}, u32[]{:S(2)}) collective-permute-start(f32[88,128]{1,0:T(8,128)S(1)} %pad_maximum_fusion), channel_id=1, source_target_pairs={{0,1},{1,2},{2,3},{3,4},{4,5},{5,6},{6,7},{7,8},{8,9},{9,10},{10,1... | collective-permute-start | bytes 135176 | tf_op jit(solution)/shard_map/ppermute | solution.py:375
  68.4 0.7 copy-start.4
